TPU v7x, 128 devices: a whole 4x4x4 slice. The times are simulated.
128 devices in a mesh: blk: 8 (over x_lo, y), grid: 16 (over x_hi, z, core).
Axes of the slice: x: 4 (x_hi: 2, x_lo: 2; x = x_hi * 2 + x_lo), y: 4, z: 4, core: 2. Of those that a mesh axis runs over, the one named last changes fastest.
Arguments:
- conn: int32 [2048, 9], P(('blk', 'grid')), may hold values from 0 to 2047, as said below
- extract: float32 [9, 9, 2048], P(None, None, ('blk', 'grid')), may hold values from 0.1 to 1
- points: float32 [3, 9, 2048], P(None, None, ('blk', 'grid')), as said below
Outputs:
- factor: float32 [1, 2048, 2, 1024], P(None, 'grid', None, 'blk')
Inputs may be any that keep to these rules, and one draw needn't show every extreme that they name: `conn`: element e = ix 32 + iy of the periodic 64 x 32 grid of elements names the functions ((ix + s) mod 64) * 32 + (iy + t) mod 32 for s, t in 0, 1, 2, each once, in an order that differs from element to element. The 9 points of element e = ix 32 + iy are the 3 x 3 Gauss points of the cell [ix / 64, (ix + 1) / 64] x [iy / 64, (iy + 1) / 64], each coordinate then moved by at most 3.5 / 64; points[2] is positive.
All inputs are finite; a program needn't handle non-finite values.
Results may differ from a plain program's by a relative error of at most 0.0003.
Values sent between devices are 32-bit elements; how exact they have to be, the bound alone decides.
A program may use at most 128 MiB of HBM per device.

v0:
```python
import math
import jax
import jax.numpy as jnp
from jax import lax
from jax.sharding import PartitionSpec as P

M = 2048
EX = 64
EY = 32
QP = 9
TB = 128
kernel_gain = 0.02
mass_shift = 0.05


def spread(array, axis, root):
    mine = lax.axis_index(axis) == root
    return lax.psum(jnp.where(mine, array, jnp.zeros_like(array)), axis)


def bernstein_table():
    spread_root = 0.5 * math.sqrt(0.6)
    gauss_nodes = [0.5 - spread_root, 0.5, 0.5 + spread_root]

    def bern_poly(which, where):
        return [(1.0 - where) ** 2, 2.0 * where * (1.0 - where), where * where][which]

    table_rows = []
    for i in range(3):
        for j in range(3):
            table_row = []
            for a in range(3):
                for b in range(3):
                    table_row.append(bern_poly(a, gauss_nodes[i]) * bern_poly(b, gauss_nodes[j]))
            table_rows.append(table_row)
    return jnp.asarray(table_rows, jnp.float32)


def torus_square(first_x, first_y, second_x, second_y):
    height = EY / EX
    gap_x = jnp.abs(first_x - second_x)
    gap_x = jnp.minimum(gap_x, jnp.abs(1.0 - gap_x))
    gap_y = jnp.abs(first_y - second_y)
    gap_y = jnp.minimum(gap_y, jnp.abs(height - gap_y))
    return gap_x * gap_x + gap_y * gap_y


def kernel_rows(test_x, test_y, trial_x, trial_y, trial_w):
    distance = torus_square(test_x[:, None], test_y[:, None], trial_x[None, :], trial_y[None, :])
    return kernel_gain * trial_w[None, :] * (1.0 + distance * (EX * EX / 4.0)) ** (-1.75)


def local_values(extract_cube):
    return jnp.einsum(
        "kb,abn->nka", bernstein_table(), extract_cube, precision=lax.Precision.HIGHEST
    )


def basis_rows(values, links):
    count = links.shape[0]
    slot = jnp.arange(count * QP, dtype=jnp.int32).reshape(count, QP)
    row_index = jnp.broadcast_to(slot[:, :, None], (count, QP, QP))
    col_index = jnp.broadcast_to(links[:, None, :], (count, QP, QP))
    return jnp.zeros((count * QP, M), jnp.float32).at[row_index, col_index].add(values)


def window_width():
    wide = 128 + 4 * EY
    return wide


def fold_window(potential_wide):
    extra = potential_wide.shape[1] - M
    return potential_wide[:, :M] + jnp.pad(potential_wide[:, M:], ((0, 0), (0, M - extra)))


def tile_target(links, grid_size, tile_rows):
    tile = links // TB
    return tile % grid_size * (tile_rows * TB) + tile // grid_size * TB + links % TB


def add_potential(state, piece, first_element, test_x, test_y):
    points_flat, extract_flat, links_flat = piece
    count = points_flat.shape[1]
    span = math.gcd(count, 128)
    width = window_width()
    window_iota = jnp.arange(width, dtype=jnp.int32)

    def step(index, inner):
        potential_wide, total = inner
        first = index * span
        part_points = lax.dynamic_slice_in_dim(points_flat, first, span, 1).reshape(3, QP, span)
        part_extract = lax.dynamic_slice_in_dim(extract_flat, first, span, 1).reshape(QP, QP, span)
        part_links = lax.dynamic_slice_in_dim(links_flat, first, span, 1).T
        kernel_block = kernel_rows(
            test_x,
            test_y,
            part_points[0].T.reshape(-1),
            part_points[1].T.reshape(-1),
            part_points[2].T.reshape(-1),
        )
        total = total + jnp.sum(kernel_block, axis=1)
        offset = (first_element + first) // EY * EY
        local = (part_links - offset) % M
        ones = (local[:, :, None] == window_iota[None, None, :]).astype(jnp.float32)
        trial_phi = jnp.einsum(
            "eka,eaw->ekw", local_values(part_extract), ones, precision=lax.Precision.HIGHEST
        ).reshape(span * QP, width)
        block = jnp.dot(
            kernel_block,
            trial_phi,
            precision=lax.Precision.HIGHEST,
            preferred_element_type=jnp.float32,
        )
        current = lax.dynamic_slice_in_dim(potential_wide, offset, width, 1)
        potential_wide = lax.dynamic_update_slice_in_dim(potential_wide, current + block, offset, 1)
        return (potential_wide, total)

    return lax.fori_loop(0, count // span, step, state)


def shards(conn, extract, points):
    count = conn.shape[0]
    rows = count * QP
    links_flat = conn.T
    extract_flat = extract.reshape(QP * QP, count)
    points_flat = points.reshape(3 * QP, count)
    own_x = points[0].T.reshape(-1)
    own_y = points[1].T.reshape(-1)
    own_w = points[2].T.reshape(-1)
    own_values = local_values(extract)
    test_phi = basis_rows(own_values, conn)
    width = window_width()
    start_state = (jnp.zeros((rows, M + width), jnp.float32), jnp.zeros((rows,), jnp.float32))
    grid_size = lax.axis_size("grid")
    blk_size = lax.axis_size("blk")
    grid_at = lax.axis_index("grid")
    blk_at = lax.axis_index("blk")
    tile_rows = M // (TB * grid_size)
    tile_cols = M // (TB * blk_size)
    band = tile_cols * TB
    potential_wide, total = add_potential(
        start_state,
        (
            lax.all_gather(points_flat, ("blk", "grid"), axis=1, tiled=True),
            lax.all_gather(extract_flat, ("blk", "grid"), axis=1, tiled=True),
            lax.all_gather(links_flat, ("blk", "grid"), axis=1, tiled=True),
        ),
        jnp.int32(0),
        own_x,
        own_y,
    )
    potential = fold_window(potential_wide)
    share = own_w[:, None] * ((mass_shift + total)[:, None] * test_phi - potential)
    own_contrib = jnp.einsum(
        "eka,ekm->eam", own_values, share.reshape(count, QP, M), precision=lax.Precision.HIGHEST
    )
    split_cols = (
        own_contrib.reshape(rows, tile_cols, blk_size, TB)
        .transpose(2, 0, 1, 3)
        .reshape(blk_size, rows, band)
    )
    targets = tile_target(conn.reshape(-1), grid_size, tile_rows)
    placed = (
        jnp.zeros((blk_size, grid_size * tile_rows * TB, band), jnp.float32)
        .at[:, targets]
        .add(split_cols)
    )
    term = placed.reshape(blk_size * grid_size, -1)
    stiff = lax.psum_scatter(term, ("blk", "grid"), scatter_dimension=0, tiled=True).reshape(
        tile_rows, TB, tile_cols, TB
    )
    column_tiles = stiff[:, :, 0, :]
    mine = spread(column_tiles, "blk", 0)
    panel_tiles = lax.all_gather(mine, "grid", axis=0, tiled=True)
    panel = panel_tiles.reshape(grid_size, tile_rows, TB, TB).transpose(1, 0, 2, 3).reshape(M, TB)
    head = panel[:TB]
    lower = jnp.linalg.cholesky(0.5 * (head + head.T))
    rest = lax.linalg.triangular_solve(
        lower, panel[TB:], left_side=False, lower=True, transpose_a=True
    )
    factor_cols = jnp.concatenate([lower, rest], axis=0)
    row_part = lax.dynamic_index_in_dim(
        factor_cols.reshape(tile_rows, grid_size, TB, TB), grid_at, 1, keepdims=False
    )
    col_part = lax.dynamic_index_in_dim(
        factor_cols.reshape(tile_cols, blk_size, TB, TB), blk_at, 1, keepdims=False
    )
    update = jnp.einsum("xuw,yvw->xuyv", row_part, col_part, precision=lax.Precision.HIGHEST)
    tile_row = (jnp.arange(tile_rows, dtype=jnp.int32) * grid_size + grid_at)[:, None, None, None]
    tile_col = (jnp.arange(tile_cols, dtype=jnp.int32) * blk_size + blk_at)[None, None, :, None]
    whole_row = tile_row * TB + jnp.arange(TB, dtype=jnp.int32)[None, :, None, None]
    whole_col = tile_col * TB + jnp.arange(TB, dtype=jnp.int32)[None, None, None, :]
    trailing = stiff - update
    result = jnp.where(
        tile_col == 0, row_part[:, :, None, :], jnp.where(tile_row == 0, 0.0, trailing)
    )
    return jnp.where(whole_row >= whole_col, result, 0.0)


def solution(mesh):
    in_specs = (
        P(("blk", "grid"), None),
        P(None, None, ("blk", "grid")),
        P(None, None, ("blk", "grid")),
    )
    out_specs = P(None, "grid", None, "blk")
    return jax.shard_map(shards, mesh=mesh, in_specs=in_specs, out_specs=out_specs, check_vma=False)
```

profile of v0, /device:TPU:1, one launch (start us, length us, event | category | flops | bytes accessed | tf_op | source)
XLA Modules:
  0.0 1185.3 jit_solution(11756267952525601225)
XLA Ops:
  13.7 182.9 %all_gather.13 = f32[81,2048]{0,1:T(8,128)S(1)} all-gather(f32[81,16]{0,1:T(8,128)S(1)} %copy.82), channel_id=1, replica_groups=mesh['blk'=8,'grid'=16] {'blk','grid'}, dimensions={1}, use_global_device_ids=true | all-gather | bytes 668736 | tf_op jit(solution)/shard_map/all_gather | solution.py:146
  197.9 183.5 %all_gather.12 = f32[27,2048]{0,1:T(8,128)} all-gather(f32[27,16]{0,1:T(8,128)S(1)} %reshape.418), channel_id=1, replica_groups=mesh['blk'=8,'grid'=16] {'blk','grid'}, dimensions={1}, use_global_device_ids=true | all-gather | bytes 222912 | tf_op jit(solution)/shard_map/all_gather | solution.py:145
  381.4 184.8 %all_gather.14 = s32[9,2048]{0,1:T(8,128)} all-gather(s32[9,16]{0,1:T(8,128)S(1)} %bitcast.107), channel_id=1, replica_groups=mesh['blk'=8,'grid'=16] {'blk','grid'}, dimensions={1}, use_global_device_ids=true | all-gather | bytes 74304 | tf_op jit(solution)/shard_map/all_gather | solution.py:147
  568.2 172.8 %while.20 = (s32[]{:T(128)}, f32[144,2304]{1,0:T(8,128)}, f32[144]{0:T(256)S(1)}, f32[27,2048]{0,1:T(8,128)}, f32[16,9]{1,0:T(8,128)}, /*index=5*/f32[16,9]{1,0:...) while((s32[]{:T(128)}, f32[144,2304]{1,0:T(8,128)}, ...), condition=%wide.wide.region_2.3_spmd.clone.clone, body=%wide.wide.region_0.2_spmd.sunk.clone.clone.sunk | while | flops 548399360 | bytes 5783860 | solution.py:119
  574.0 2.4 convolution_add_fusion.3
  584.8 2.4 convolution_add_fusion.3
  587.2 1.7 dynamic_update_slice.15
  595.7 2.4 convolution_add_fusion.3
  606.5 2.4 convolution_add_fusion.3
  617.3 2.4 convolution_add_fusion.3
  628.0 2.4 convolution_add_fusion.3
  638.8 2.4 convolution_add_fusion.3
  649.6 2.4 convolution_add_fusion.3
  660.5 2.4 convolution_add_fusion.3
  671.3 2.4 convolution_add_fusion.3
  682.1 2.4 convolution_add_fusion.3
  692.9 2.4 convolution_add_fusion.3
  703.7 2.4 convolution_add_fusion.3
  714.5 2.4 convolution_add_fusion.3
  725.3 2.4 convolution_add_fusion.3
  736.1 2.4 convolution_add_fusion.3
  745.1 10.7 scatter_custom_fusion.1
  759.3 3.3 fusion.33
  764.3 6.0 broadcast_in_dim.83
  770.3 16.2 %scatter_fusion = f32[8,2048,256]{2,0,1:T(8,128)} fusion(f32[8,2048,256]{2,0,1:T(8,128)} %broadcast_in_dim.83, s32[144]{0:T(256)S(1)} %bitcast.113, f32[144,8,256]{2,1,0:T(8,128)S(1)} %bitcast.99), kind=kCustom, calls=%fused_computation | custom fusion | flops 294912 | bytes 3539520 | tf_op jit(solution)/shard_map/scatter-add | solution.py:167
  786.4 15.8 %copy.93 = f32[8,2048,256]{2,1,0:T(8,128)} copy(f32[8,2048,256]{2,0,1:T(8,128)} %scatter_fusion) | data formatting | bytes 33554432 | tf_op jit(solution)/shard_map/scatter-add | solution.py:167
  802.3 18.2 %reshape.386 = f32[128,32768]{1,0:T(8,128)} reshape(f32[8,2048,256]{2,1,0:T(8,128)} %copy.93) | data formatting | bytes 33554432 | tf_op jit(solution)/shard_map/reshape | solution.py:169
  820.6 210.2 %all-reduce.7.cloned.1.call-done = f32[128,32768]{1,0:T(8,128)} async-done(((f32[128,32768]{1,0:T(8,128)}), f32[128,32768]{1,0:T(8,128)}) %all-reduce.7.cloned.1.call-update) | async-done | bytes 16777232
  1033.1 66.6 %all-reduce.5.cloned.1.call-done = f32[1,128,128]{2,1,0:T(8,128)} async-done(((f32[1,128,128]{2,1,0:T(8,128)}), f32[1,128,128]{2,1,0:T(8,128)}) %all-reduce.5.cloned.1.call-update) | async-done | bytes 65552 | tf_op jit(solution)/shard_map/psum | solution.py:18
  1099.9 52.0 %all-gather.2.cloned.1.call-done = f32[16,128,128]{2,1,0:T(8,128)} async-done(((f32[1,128,128]{2,1,0:T(8,128)}), f32[16,128,128]{2,1,0:T(8,128)}) %all-gather.2.cloned.1.call-update) | async-done | bytes 1048592 | tf_op jit(solution)/shard_map/all_gather | solution.py:175
  1153.8 11.7 cholesky.18
  1166.9 9.8 custom-call.6
  (313 shorter events, 158.2 us)
Async XLA Ops:
  6.5 1024.2 %all-reduce.7.cloned.1.call-start = ((), (), s32[]{:S(2)}) async-start(), calls=%async_computation.2 | async-start | bytes 33554432
  12.4 185.4 %copy-start.4 = (f32[1,9,16]{1,2,0:T(8,128)}, f32[1,9,16]{1,2,0:T(8,128)S(1)}, u32[]{:S(2)}) copy-start(f32[1,9,16]{1,2,0:T(8,128)S(1)} %copy.103) | copy-start | bytes 1732
  12.6 185.2 %copy-start.5 = (f32[1,9,16]{1,2,0:T(8,128)}, f32[1,9,16]{1,2,0:T(8,128)S(1)}, u32[]{:S(2)}) copy-start(f32[1,9,16]{1,2,0:T(8,128)S(1)} %copy.102) | copy-start | bytes 1732
  196.6 184.8 %copy-start.3 = (s32[16,9]{1,0:T(8,128)S(1)}, s32[16,9]{1,0:T(8,128)}, u32[]{:S(2)}) copy-start(s32[16,9]{1,0:T(8,128)} %param.7) | copy-start | bytes 1732
  197.8 368.3 %copy-start.1 = (f32[9,9,1]{1,0,2:T(8,128)S(1)}, f32[9,9,1]{1,0,2:T(8,128)}, u32[]{:S(2)}) copy-start(f32[9,9,1]{1,0,2:T(8,128)} %constant.314) | copy-start | bytes 976
  197.8 368.3 %copy-start.2 = (f32[9,9,16]{2,1,0:T(8,128)S(1)}, f32[9,9,16]{2,1,0:T(8,128)}, u32[]{:S(2)}) copy-start(f32[9,9,16]{2,1,0:T(8,128)} %param.8) | copy-start | bytes 15556
  568.2 174.9 %copy-start.9 = (s32[2]{0:T(128)S(1)}, s32[2]{0:T(128)}, u32[]{:S(2)}) copy-start(s32[2]{0:T(128)} %constant.303) | copy-start | bytes 28
  568.2 175.1 %copy-start.8 = (s32[2]{0:T(128)S(1)}, s32[2]{0:T(128)}, u32[]{:S(2)}) copy-start(s32[2]{0:T(128)} %constant.306) | copy-start | bytes 28
  755.8 1.2 copy-start.6
  755.9 1.8 copy-start
  762.6 1.6 copy-start.7
  820.5 279.2 %all-reduce.5.cloned.1.call-start = ((), (), s32[]{:S(2)}) async-start(), calls=%async_computation | async-start | bytes 131072 | tf_op jit(solution)/shard_map/psum | solution.py:18
  1032.8 119.1 %all-gather.2.cloned.1.call-start = ((), (), s32[]{:S(2)}) async-start(), calls=%async_computation.1 | async-start | bytes 1114112 | tf_op jit(solution)/shard_map/all_gather | solution.py:175
  1153.7 23.0 %slice-start = ((f32[16,128,128]{2,1,0:T(8,128)}), f32[15,128,128]{2,1,0:T(8,128)S(1)}, s32[]{:S(2)}) async-start(f32[16,128,128]{2,1,0:T(8,128)} %all-gather.2.cloned.1.call-done), calls=%async_computation.3 | async-start | bytes 1966080 | tf_op jit(solution)/shard_map/slice | solution.py:180
Sparse Core Ops, SparseCore 0:
  820.6 210.1 all-reduce.6
  1033.4 66.3 all-reduce.4
  1102.2 49.6 all-gather.1
where the time goes:
time: 1190 us
  blocking collectives  551 us (46%)
  waiting for transfers between devices  329 us (28%)
  local copies, waits for them, and re-layouts  120 us (10%)
  other arithmetic  99.5 us (8%)
  matrix products  70.7 us (6%)
  between operations  13.4 us (1%)
    unnamed x4, waiting for transfers between devices  210 us
    all_gather x1, blocking collectives, shards(): lax.all_gather(links_flat, ('blk', 'grid'), axis=1, tiled=True)  185 us
    all_gather x1, blocking collectives, shards(): lax.all_gather(points_flat, ('blk', 'grid'), axis=1, tiled=True)  183 us
    all_gather x1, blocking collectives, shards(): lax.all_gather(extract_flat, ('blk', 'grid'), axis=1, tiled=True)  183 us
    psum x1, waiting for transfers between devices, spread(): return lax.psum(jnp.where(mine, array, jnp.zeros_like(array)), axis)  66.6 us
    all_gather x1, waiting for transfers between devices, shards(): panel_tiles = lax.all_gather(mine, 'grid', axis=0, tiled=True)  52 us
    dot_general x16, matrix products, step(): jnp.dot(kernel_block, trial_phi, precision=lax.Precision.HIGHEST, preferr...  38.3 us
    dynamic_update_slice x16, local copies, waits for them, and re-layouts, step(): lax.dynamic_update_slice_in_dim(potential_wide, current + block, offset, 1)  27.4 us
  transfers between devices with their start and end apart: 3, of which 3 were waited for; matrix products, arithmetic and copies ran while one was open for 0% of the time, Pallas kernels for 0%

commit v1 on v0

--- a/solution.py
+++ b/solution.py
@@ -144,7 +144,12 @@
         (
             lax.all_gather(points_flat, ("blk", "grid"), axis=1, tiled=True),
             lax.all_gather(extract_flat, ("blk", "grid"), axis=1, tiled=True),
-            lax.all_gather(links_flat, ("blk", "grid"), axis=1, tiled=True),
+            jnp.concatenate(
+                lax.all_to_all(
+                    jnp.stack([links_flat] * lax.axis_size(("blk", "grid"))), ("blk", "grid"), 0, 0
+                ),
+                axis=1,
+            ),
         ),
         jnp.int32(0),
         own_x,

time: 1190 us -> 1010 us (0.85)
  blocking collectives: 551 us -> 365 us
    all_gather x1 -> x0, blocking collectives: 185 us -> none  [shards(): lax.all_gather(links_flat, ('blk', 'grid'), axis=1, tiled=True)]
  transfers between devices with their start and end apart: 3 -> 4, of which waited for: 3 -> 3; matrix products, arithmetic and copies ran while one was open for 0% -> 2% of each run, Pallas kernels for 0% -> 0%
where the time goes in v1:
time: 1010 us
  blocking collectives  365 us (36%)
  waiting for transfers between devices  330 us (33%)
  local copies, waits for them, and re-layouts  118 us (12%)
  other arithmetic  98.6 us (10%)
  matrix products  70 us (7%)
  between operations  13.5 us (1%)
  starting transfers between devices  11.8 us (1%)
    unnamed x4, waiting for transfers between devices  211 us
    all_gather x1, blocking collectives, shards(): lax.all_gather(points_flat, ('blk', 'grid'), axis=1, tiled=True)  184 us
    all_gather x1, blocking collectives, shards(): lax.all_gather(extract_flat, ('blk', 'grid'), axis=1, tiled=True)  181 us
    psum x1, waiting for transfers between devices, spread(): return lax.psum(jnp.where(mine, array, jnp.zeros_like(array)), axis)  66.6 us
    all_gather x1, waiting for transfers between devices, shards(): panel_tiles = lax.all_gather(mine, 'grid', axis=0, tiled=True)  52 us
    dot_general x16, matrix products, step(): jnp.dot(kernel_block, trial_phi, precision=lax.Precision.HIGHEST, preferr...  38.3 us
    dynamic_update_slice x16, local copies, waits for them, and re-layouts, step(): lax.dynamic_update_slice_in_dim(potential_wide, current + block, offset, 1)  27.4 us
    dot_general x16, matrix products, step(): jnp.einsum('eka,eaw->ekw', local_values(part_extract), ones, precision=la...  23.8 us
  transfers between devices with their start and end apart: 4, of which 3 were waited for; matrix products, arithmetic and copies ran while one was open for 2% of the time, Pallas kernels for 0%

profile of v1, /device:TPU:1, one launch (start us, length us, event | category | flops | bytes accessed | tf_op | source)
XLA Modules:
  0.0 1008.1 jit_solution(8382467382901378249)
XLA Ops:
  8.8 11.5 %all-to-all-start = ((s32[128,1,144]{2,1,0:T(1,128)}), s32[128,1,144]{2,1,0:T(1,128)S(1)}, u32[]{:S(2)}, u32[]{:S(2)}) async-start(s32[128,1,144]{2,1,0:T(1,128)} %reshape.431), calls=%async_computation | async-start | bytes 262144 | tf_op jit(solution)/shard_map/all_to_all | solution.py:148
  21.2 181.1 %all_gather.10 = f32[81,2048]{0,1:T(8,128)S(1)} all-gather(f32[81,16]{0,1:T(8,128)S(1)} %copy.82), channel_id=1, replica_groups=mesh['blk'=8,'grid'=16] {'blk','grid'}, dimensions={1}, use_global_device_ids=true | all-gather | bytes 668736 | tf_op jit(solution)/shard_map/all_gather | solution.py:146
  205.5 10.5 %scatter_custom_fusion.1 = f32[294912]{0:T(1024)S(1)} fusion(s32[1296]{0:T(1024)S(1)} %reshape.417, f32[1296]{0:T(1024)S(1)} %reshape.419, f32[]{:T(128)} %constant.282.clone.1), kind=kCustom, calls=%fused_computation.32 | custom fusion | flops 1296 | bytes 1179652
  217.5 183.5 %all_gather.9 = f32[27,2048]{0,1:T(8,128)} all-gather(f32[27,16]{0,1:T(8,128)S(1)} %reshape.428), channel_id=1, replica_groups=mesh['blk'=8,'grid'=16] {'blk','grid'}, dimensions={1}, use_global_device_ids=true | all-gather | bytes 222912 | tf_op jit(solution)/shard_map/all_gather | solution.py:145
  405.3 172.8 %while.20 = (s32[]{:T(128)}, f32[144,2304]{1,0:T(8,128)}, f32[144]{0:T(256)S(1)}, f32[27,2048]{0,1:T(8,128)}, f32[16,9]{1,0:T(8,128)}, /*index=5*/f32[16,9]{1,0:...) while((s32[]{:T(128)}, f32[144,2304]{1,0:T(8,128)}, ...), condition=%wide.wide.region_2.3_spmd.clone.clone, body=%wide.wide.region_0.2_spmd.sunk.clone.clone.sunk | while | flops 548399360 | bytes 5783860 | solution.py:119
  411.1 2.4 convolution_add_fusion.3
  421.9 2.4 convolution_add_fusion.3
  432.7 2.4 convolution_add_fusion.3
  443.5 2.4 convolution_add_fusion.3
  454.3 2.4 convolution_add_fusion.3
  465.1 2.4 convolution_add_fusion.3
  475.9 2.4 convolution_add_fusion.3
  486.7 2.4 convolution_add_fusion.3
  497.5 2.4 convolution_add_fusion.3
  508.3 2.4 convolution_add_fusion.3
  519.2 2.4 convolution_add_fusion.3
  530.0 2.4 convolution_add_fusion.3
  540.8 2.4 convolution_add_fusion.3
  551.6 2.4 convolution_add_fusion.3
  562.4 2.4 convolution_add_fusion.3
  573.2 2.4 convolution_add_fusion.3
  579.0 1.9 subtract_multiply_fusion
  581.1 3.3 fusion.33
  586.0 6.0 broadcast_in_dim.83
  592.0 16.2 %scatter_fusion = f32[8,2048,256]{2,0,1:T(8,128)} fusion(f32[8,2048,256]{2,0,1:T(8,128)} %broadcast_in_dim.83, s32[144]{0:T(256)S(1)} %bitcast.119, f32[144,8,256]{2,1,0:T(8,128)S(1)} %bitcast.105), kind=kCustom, calls=%fused_computation | custom fusion | flops 294912 | bytes 3539520 | tf_op jit(solution)/shard_map/scatter-add | solution.py:172
  608.2 15.8 %copy.93 = f32[8,2048,256]{2,1,0:T(8,128)} copy(f32[8,2048,256]{2,0,1:T(8,128)} %scatter_fusion) | data formatting | bytes 33554432 | tf_op jit(solution)/shard_map/scatter-add | solution.py:172
  624.0 18.2 %reshape.396 = f32[128,32768]{1,0:T(8,128)} reshape(f32[8,2048,256]{2,1,0:T(8,128)} %copy.93) | data formatting | bytes 33554432 | tf_op jit(solution)/shard_map/reshape | solution.py:174
  642.3 211.3 %all-reduce.7.cloned.1.call-done = f32[128,32768]{1,0:T(8,128)} async-done(((f32[128,32768]{1,0:T(8,128)}), f32[128,32768]{1,0:T(8,128)}) %all-reduce.7.cloned.1.call-update) | async-done | bytes 16777232
  855.9 66.6 %all-reduce.5.cloned.1.call-done = f32[1,128,128]{2,1,0:T(8,128)} async-done(((f32[1,128,128]{2,1,0:T(8,128)}), f32[1,128,128]{2,1,0:T(8,128)}) %all-reduce.5.cloned.1.call-update) | async-done | bytes 65552 | tf_op jit(solution)/shard_map/psum | solution.py:18
  922.7 52.0 %all-gather.2.cloned.1.call-done = f32[16,128,128]{2,1,0:T(8,128)} async-done(((f32[1,128,128]{2,1,0:T(8,128)}), f32[16,128,128]{2,1,0:T(8,128)}) %all-gather.2.cloned.1.call-update) | async-done | bytes 1048592 | tf_op jit(solution)/shard_map/all_gather | solution.py:180
  976.6 11.7 %cholesky.18 = f32[128,128]{1,0:T(8,128)S(1)} custom-call(f32[128,128]{1,0:T(8,128)S(1)} %fusion.23), custom_call_target="Cholesky" | custom-call | tf_op jit(solution)/shard_map/jit(cholesky)/cholesky | solution.py:183
  989.7 9.8 custom-call.6
  (314 shorter events, 155.0 us)
Async XLA Ops:
  6.5 14.0 %copy-start.2 = (s32[16,9]{1,0:T(8,128)S(1)}, s32[16,9]{1,0:T(8,128)}, u32[]{:S(2)}) copy-start(s32[16,9]{1,0:T(8,128)} %param.7) | copy-start | bytes 1732
  6.5 13.8 %copy-start.3 = (f32[3,9,16]{2,0,1:T(4,128)S(1)}, f32[3,9,16]{2,0,1:T(4,128)}, u32[]{:S(2)}) copy-start(f32[3,9,16]{2,0,1:T(4,128)} %param.9) | copy-start | bytes 5188
  6.5 14.5 %copy-start.1 = (f32[9,9,16]{2,1,0:T(8,128)S(1)}, f32[9,9,16]{2,1,0:T(8,128)}, u32[]{:S(2)}) copy-start(f32[9,9,16]{2,1,0:T(8,128)} %param.8) | copy-start | bytes 15556
  8.8 392.2 %all-to-all-start = ((s32[128,1,144]{2,1,0:T(1,128)}), s32[128,1,144]{2,1,0:T(1,128)S(1)}, u32[]{:S(2)}, u32[]{:S(2)}) async-start(s32[128,1,144]{2,1,0:T(1,128)} %reshape.431), calls=%async_computation | async-start | bytes 262144 | tf_op jit(solution)/shard_map/all_to_all | solution.py:148
  20.3 833.3 %all-reduce.7.cloned.1.call-start = ((), (), s32[]{:S(2)}) async-start(), calls=%async_computation.3 | async-start | bytes 33554432
  20.8 182.7 %copy-start.4 = (f32[1,9,16]{1,2,0:T(8,128)}, f32[1,9,16]{1,2,0:T(8,128)S(1)}, u32[]{:S(2)}) copy-start(f32[1,9,16]{1,2,0:T(8,128)S(1)} %copy.103) | copy-start | bytes 1732
  21.0 182.5 %copy-start.5 = (f32[1,9,16]{1,2,0:T(8,128)}, f32[1,9,16]{1,2,0:T(8,128)S(1)}, u32[]{:S(2)}) copy-start(f32[1,9,16]{1,2,0:T(8,128)S(1)} %copy.102) | copy-start | bytes 1732
  21.2 182.9 %copy-start.7 = (s32[2]{0:T(128)S(1)}, s32[2]{0:T(128)}, u32[]{:S(2)}) copy-start(s32[2]{0:T(128)} %constant.303) | copy-start | bytes 28
  202.3 2.0 copy-start.6
  202.3 2.7 copy-start
  642.2 280.3 %all-reduce.5.cloned.1.call-start = ((), (), s32[]{:S(2)}) async-start(), calls=%async_computation.1 | async-start | bytes 131072 | tf_op jit(solution)/shard_map/psum | solution.py:18
  855.6 119.1 %all-gather.2.cloned.1.call-start = ((), (), s32[]{:S(2)}) async-start(), calls=%async_computation.2 | async-start | bytes 1114112 | tf_op jit(solution)/shard_map/all_gather | solution.py:180
  976.5 23.0 %slice-start = ((f32[16,128,128]{2,1,0:T(8,128)}), f32[15,128,128]{2,1,0:T(8,128)S(1)}, s32[]{:S(2)}) async-start(f32[16,128,128]{2,1,0:T(8,128)} %all-gather.2.cloned.1.call-done), calls=%async_computation.4 | async-start | bytes 1966080 | tf_op jit(solution)/shard_map/slice | solution.py:185
Sparse Core Ops, SparseCore 0:
  642.4 211.1 all-reduce.6
  856.2 66.3 all-reduce.4
  925.0 49.6 all-gather.1
